TPU v7x, 1024 devices: a whole 4x8x16 slice. The times are simulated.
1024 devices in a mesh: wide: 128 (over y, z), narrow: 8 (over x, core).
Axes of the slice: x: 4, y: 8, z: 16, core: 2. Of those that a mesh axis runs over, the one named last changes fastest.
Arguments:
- tiles: float32 [128, 48, 256, 256], P('wide', 'narrow'), may hold values from -12 to 12, as said below
- tile_rows: int32 [128, 48], P('wide', 'narrow'), may hold values from 0 to 511, as said below
- tile_cols: int32 [128, 48], P('wide', 'narrow'), may hold values from 0 to 511, as said below
- tile_counts: int32 [128, 8], P('wide', 'narrow'), may hold values from 0 to 6, as said below
Outputs:
- scaled_tiles: float32 [128, 48, 256, 256], P('wide', 'narrow')
- scaling: float32 [512, 256], P('wide')
Inputs may be any that keep to these rules, and one draw needn't show every extreme that they name: `tile_rows`: A live slot of device (w, n) names a block row in w * 4 to (w + 1) * 4 - 1, and every block row has exactly one live diagonal tile, on the device whose block columns hold it. Unused slots name block row w * 4. `tile_cols`: A live slot of device (w, n) names a block column in n * 64 to (n + 1) * 64 - 1, not below its block row; no tile is stored twice. Unused slots name block column n * 64. `tile_counts`: the device that holds a block row's diagonal tile uses all slots. Diagonal tiles are symmetric with diagonal entries in 0.3 to 1.5.
All inputs are finite; a program needn't handle non-finite values.
Results may differ from a plain program's by a relative error of at most 0.00002.
Values sent between devices are 32-bit elements; how exact they have to be, the bound alone decides.
A program may use at most 32 MiB of HBM per device.

v0:
```python
import jax
import jax.numpy as jnp
from jax import lax
from jax.sharding import PartitionSpec as P

TILE = 256
ROWB = 4
ITERS = 2


def from_root(block, axis, owner):
    block = jnp.where(lax.axis_index(axis) == owner, block, jnp.zeros_like(block))
    return lax.psum(block, axis)


def on_device(tiles, tile_rows, tile_cols, tile_counts):
    wide_size = lax.axis_size("wide")
    narrow_size = lax.axis_size("narrow")
    column_blocks = ROWB * wide_size // narrow_size
    slot_count = tiles.shape[1]
    wide_index = lax.axis_index("wide")
    narrow_index = lax.axis_index("narrow")
    blocks = tiles[0]
    magnitude = jnp.abs(blocks)
    row_local = tile_rows[0] - wide_index * ROWB
    col_local = tile_cols[0] - narrow_index * column_blocks
    live_slots = jnp.arange(slot_count) < tile_counts[0, 0]
    col_target = jnp.where(live_slots, col_local, 0)
    offset = wide_index * ROWB - narrow_index * column_blocks
    inside = (offset >= 0) & (offset < column_blocks)
    start_block = jnp.clip(offset, 0, column_blocks - ROWB)
    home_index = wide_index * ROWB // column_blocks
    row_scale = jnp.ones((ROWB, TILE), jnp.float32)
    col_scale = jnp.ones((column_blocks, TILE), jnp.float32)
    for iteration in range(ITERS):
        left_scale = row_scale[row_local]
        right_scale = col_scale[col_local]
        scaled = magnitude * left_scale[:, :, None] * right_scale[:, None, :]
        scaled = jnp.where(live_slots[:, None, None], scaled, jnp.float32(0.0))
        row_peak = jnp.max(scaled, axis=2)
        col_peak = jnp.max(scaled, axis=1)
        row_part = jnp.zeros((ROWB, TILE), jnp.float32).at[row_local].max(row_peak)
        row_full = lax.pmax(row_part, "narrow")
        own_rows = jnp.where(inside, row_full, jnp.float32(0.0))
        empty_columns = jnp.zeros((column_blocks, TILE), jnp.float32)
        col_part = empty_columns.at[col_target].max(col_peak)
        window = lax.dynamic_slice_in_dim(col_part, start_block, ROWB, 0)
        col_part = lax.dynamic_update_slice_in_dim(
            col_part, jnp.maximum(window, own_rows), start_block, 0
        )
        col_full = lax.pmax(col_part, "wide")
        row_window = lax.dynamic_slice_in_dim(col_full, start_block, ROWB, 0)
        row_total = from_root(row_window, "narrow", home_index)
        row_scale = row_scale / jnp.sqrt(row_total)
        col_scale = col_scale / jnp.sqrt(col_full)
    left_scale = row_scale[row_local]
    right_scale = col_scale[col_local]
    result = blocks * left_scale[:, :, None] * right_scale[:, None, :]
    result = jnp.where(live_slots[:, None, None], result, jnp.float32(0.0))
    return (result[None], row_scale)


def solution(mesh):
    placed = (
        P("wide", "narrow", None, None),
        P("wide", "narrow"),
        P("wide", "narrow"),
        P("wide", "narrow"),
    )
    return jax.shard_map(
        on_device,
        mesh=mesh,
        in_specs=placed,
        out_specs=(P("wide", "narrow", None, None), P("wide", None)),
        check_vma=False,
    )
```

profile of v0, /device:TPU:1, one launch (start us, length us, event | category | flops | bytes accessed | tf_op | source)
XLA Modules:
  0.0 621.4 jit_solution(9367537706964917345)
XLA Ops:
  8.0 0.7 fusion.17
  8.7 0.6 gather_fusion
  9.3 0.6 gather_fusion.1
  9.9 2.0 fusion.6
  11.9 0.6 scatter_custom_fusion.1
  12.5 25.9 %pmax.28 = f32[4,256]{1,0:T(4,128)S(1)} all-reduce(f32[4,256]{1,0:T(4,128)S(1)} %scatter_custom_fusion.1), channel_id=1, replica_groups=mesh['wide'=128,'narrow'=8] {'narrow'}, use_global_device_ids=true, to_apply=%region_4.5 | all-reduce | flops 1024 | bytes 8192 | tf_op jit(solution)/shard_map/pmax | solution.py:43
  38.4 0.6 scatter_custom_fusion
  39.2 0.6 copy-done.4
  40.0 255.6 %all-reduce.3.cloned.1.call-done = f32[64,256]{1,0:T(8,128)} async-done(((f32[64,256]{1,0:T(8,128)}), f32[64,256]{1,0:T(8,128)}) %all-reduce.3.cloned.1.call-update) | async-done | bytes 65552 | tf_op jit(solution)/shard_map/pmax | solution.py:51
  295.5 0.8 dynamic-slice_select_fusion.1
  296.3 23.2 %psum.14 = f32[4,256]{1,0:T(4,128)S(1)} all-reduce(f32[4,256]{1,0:T(4,128)S(1)} %dynamic-slice_select_fusion.1), channel_id=1, replica_groups=mesh['wide'=128,'narrow'=8] {'narrow'}, use_global_device_ids=true, to_apply=%region_6.7 | all-reduce | flops 1024 | bytes 8192 | tf_op jit(solution)/shard_map/psum | solution.py:13
  319.5 0.6 gather_fusion.2
  320.0 0.9 sqrt.13
  320.9 0.6 gather_fusion.3
  321.5 0.7 fusion.4
  322.2 0.6 scatter_custom_fusion.3
  322.8 12.4 %pmax.30 = f32[4,256]{1,0:T(4,128)S(1)} all-reduce(f32[4,256]{1,0:T(4,128)S(1)} %scatter_custom_fusion.3), channel_id=1, replica_groups=mesh['wide'=128,'narrow'=8] {'narrow'}, use_global_device_ids=true, to_apply=%region_11.12 | all-reduce | flops 1024 | bytes 8192 | tf_op jit(solution)/shard_map/pmax | solution.py:43
  335.2 0.6 scatter_custom_fusion.2
  336.1 0.6 copy-done.3
  336.7 250.5 %all-reduce.5.cloned.1.call-done = f32[64,256]{1,0:T(8,128)} async-done(((f32[64,256]{1,0:T(8,128)}), f32[64,256]{1,0:T(8,128)}) %all-reduce.5.cloned.1.call-update) | async-done | bytes 65552 | tf_op jit(solution)/shard_map/pmax | solution.py:51
  587.2 0.9 rsqrt_multiply_fusion
  588.6 0.7 dynamic-slice_select_fusion
  589.4 23.2 %psum.15 = f32[4,256]{1,0:T(4,128)S(1)} all-reduce(f32[4,256]{1,0:T(4,128)S(1)} %dynamic-slice_select_fusion), channel_id=1, replica_groups=mesh['wide'=128,'narrow'=8] {'narrow'}, use_global_device_ids=true, to_apply=%region_13.14 | all-reduce | flops 1024 | bytes 8192 | tf_op jit(solution)/shard_map/psum | solution.py:13
  613.1 1.4 multiply_select_fusion
  (25 shorter events, 1.6 us)
Async XLA Ops:
  7.2 314.3 %copy-start = (f32[1,6,256,256]{3,2,1,0:T(8,128)S(1)}, f32[1,6,256,256]{3,2,1,0:T(8,128)}, u32[]{:S(2)}) copy-start(f32[1,6,256,256]{3,2,1,0:T(8,128)} %param.4) | copy-start | bytes 4718596
  7.2 288.3 %all-reduce.3.cloned.1.call-start = ((), (), s32[]{:S(2)}) async-start(), calls=%async_computation | async-start | bytes 131072 | tf_op jit(solution)/shard_map/pmax | solution.py:51
  39.2 0.6 copy-start.4
  39.9 547.3 %all-reduce.5.cloned.1.call-start = ((), (), s32[]{:S(2)}) async-start(), calls=%async_computation.1 | async-start | bytes 131072 | tf_op jit(solution)/shard_map/pmax | solution.py:51
  295.5 291.7 %copy-start.2 = (f32[64,256]{1,0:T(8,128)S(1)}, f32[64,256]{1,0:T(8,128)}, u32[]{:S(2)}) copy-start(f32[64,256]{1,0:T(8,128)} %all-reduce.3.cloned.1.call-done) | copy-start | bytes 196612
  336.1 0.6 copy-start.3
  612.5 2.0 copy-start.1
Sparse Core Ops, SparseCore 0:
  40.0 255.4 all-reduce.2
  336.8 250.3 all-reduce.4
where the time goes:
time: 622 us; the launch traced here: 621 us
  waiting for transfers between devices  506 us (81%)
  blocking collectives  84.6 us (14%)
  between operations  15 us (2%)
  other arithmetic  9.81 us (2%)
    pmax x2, waiting for transfers between devices, on_device(): col_full = lax.pmax(col_part, 'wide')  506 us
    psum x2, blocking collectives, from_root(): return lax.psum(block, axis)  46.3 us
    pmax x2, blocking collectives, on_device(): row_full = lax.pmax(row_part, 'narrow')  38.3 us
  transfers between devices with their start and end apart: 2, of which 2 were waited for; matrix products, arithmetic and copies ran while one was open for 0% of the time, Pallas kernels for 0%

commit v1 on v0

v1 whole, which is shorter than its diff:
```python
import jax
import jax.numpy as jnp
from jax import lax
from jax.experimental import pallas as pl
from jax.experimental.pallas import tpu as pltpu
from jax.sharding import PartitionSpec as P

TILE = 256
ROWB = 4
ITERS = 2
LANES = 128
SLOTS = 6
Y, Z, N = 8, 16, 8
MESH = pl.DeviceIdType.MESH
FAR_Z = (8, 7, 9, 6, 10, 5, 11, 4, 12, 3, 13, 2, 14, 1, 15)
FAR_8 = (4, 3, 5, 2, 6, 1, 7)


def place():
    wide = lax.axis_index("wide")
    return wide, wide // Z, lax.rem(wide, Z), lax.axis_index("narrow")


def remote(src, dst, send, recv, device):
    return pltpu.make_async_remote_copy(
        src_ref=src, dst_ref=dst, send_sem=send, recv_sem=recv,
        device_id=device, device_id_type=MESH,
    )


def half_rows(peaks):
    sub = lax.broadcasted_iota(jnp.int32, (8, LANES), 0)
    shape = (8, LANES)
    return jnp.where(
        lax.rem(sub, 2) == 0,
        jnp.broadcast_to(peaks[0], shape),
        jnp.broadcast_to(peaks[1], shape),
    )


def row_peaks(left_half, right_half):
    widest = jnp.maximum(left_half, right_half)
    return [
        jnp.max(widest[h * LANES:(h + 1) * LANES].T, axis=0, keepdims=True)
        for h in range(2)
    ]


def kernel(
    rows_ref, cols_ref, count_ref, tiles_ref,
    left_ref, right_ref, scaling_ref,
    tile, size, rsub, colp, rowp, rowacc, nrecv, zrecv, ypart, yrecv, own, cs_1, cs_2, rs_1, rs_2,
    tsem, zs, zr, gs, gr, ys, yr, ns, nr, bs, br,
):
    wide, y, z, n = place()
    owner = n == y
    cs, rs = (cs_1, cs_2), (rs_1, rs_2)
    z_peers = [(y * Z + lax.rem(z + d, Z), n) for d in FAR_Z]
    y_peers = [(lax.rem(y + d, Y) * Z + z, n) for d in FAR_8]
    n_peers = [(wide, lax.rem(n + d, N)) for d in FAR_8]

    barrier = pltpu.get_barrier_semaphore()
    for peer in z_peers + y_peers + n_peers:
        pl.semaphore_signal(barrier, inc=1, device_id=peer, device_id_type=MESH)
    loads = [
        pltpu.make_async_copy(tiles_ref.at[0, s], tile.at[s], tsem.at[s])
        for s in range(SLOTS)
    ]
    for load in loads:
        load.start()

    count = count_ref[0, 0]
    row_of = [
        jnp.clip(rows_ref[0, s] - wide * ROWB, 0, ROWB - 1) for s in range(SLOTS)
    ]
    col_of = [
        jnp.clip(cols_ref[0, s] - n * (ROWB * Z), 0, ROWB * Z - 1) for s in range(SLOTS)
    ]
    row_live = [jnp.where(s < count, row_of[s], -1) for s in range(SLOTS)]
    col_live = [jnp.where(s < count, col_of[s], -1) for s in range(SLOTS)]
    row_id = lax.broadcasted_iota(jnp.int32, (8, LANES), 0) // 2
    col_id = (
        lax.broadcasted_iota(jnp.int32, (Z, 8, LANES), 0) * ROWB
        + lax.broadcasted_iota(jnp.int32, (Z, 8, LANES), 1) // 2
    )

    def add_rows(total, s, peaks):
        return jnp.maximum(
            total, jnp.where(row_id == row_live[s], half_rows(peaks), 0.0)
        )

    def add_cols(total, s, peaks):
        return jnp.maximum(
            total, jnp.where(col_id == col_live[s], half_rows(peaks)[None], 0.0)
        )

    def scatter_columns(it):
        copies = []
        for i, d in enumerate(FAR_Z):
            copy = remote(
                colp.at[it, lax.rem(z + d, Z)], zrecv.at[it, i],
                zs.at[it, i], zr.at[it, i], z_peers[i],
            )
            copy.start()
            copies.append(copy)
        return copies

    def row_copy(it, slot, device):
        return remote(
            rowp.at[it], nrecv.at[it, slot], ns.at[it], nr.at[it, slot], device
        )

    def send_rows(it):
        @pl.when(jnp.logical_not(owner))
        def _():
            row_copy(it, lax.rem(n - y + N, N) - 1, (wide, y)).start()

    def reduce_rows(it):
        @pl.when(owner)
        def _():
            total = rowp[it]
            for i in range(N - 1):
                row_copy(it, i, n_peers[0]).wait_recv()
                total = jnp.maximum(total, nrecv[it, i])
            rowacc[...] = total

        @pl.when(jnp.logical_not(owner))
        def _():
            rowacc[...] = jnp.zeros((8, LANES), jnp.float32)

    def reduce_chunk(it, copies):
        total = colp[it, z]
        for i, copy in enumerate(copies):
            copy.wait_recv()
            total = jnp.maximum(total, zrecv[it, i])
        return total

    def reduce_y(it, part):
        ypart[it] = part
        copies = []
        for i in range(Y - 1):
            copy = remote(
                ypart.at[it], yrecv.at[it, i], ys.at[it, i], yr.at[it, i], y_peers[i]
            )
            copy.start()
            copies.append(copy)
        for i, copy in enumerate(copies):
            copy.wait_recv()
            part = jnp.maximum(part, yrecv[it, i])
        return part, copies

    def scale_copy(it, i):
        return remote(own.at[it], rs[it], bs.at[it, i], br.at[it], n_peers[i])

    def spread(it, scale):
        own[it] = scale
        mine = pl.ds(pl.multiple_of(z * 8, 8), 8)

        @pl.when(owner)
        def _():
            for i in range(N - 1):
                scale_copy(it, i).start()

        copies = []
        for i in range(Z - 1):
            copy = remote(
                own.at[it], cs[it].at[mine], gs.at[it, i], gr.at[it, i], z_peers[i]
            )
            copy.start()
            copies.append(copy)
        cs[it][mine] = scale

        @pl.when(owner)
        def _():
            rs[it][...] = scale

        @pl.when(jnp.logical_not(owner))
        def _():
            scale_copy(it, 0).wait_recv()

        return copies

    def await_columns(it, copies):
        for i, d in enumerate(FAR_Z):
            sender = lax.rem(z + Z - d, Z)
            there = pl.ds(pl.multiple_of(sender * 8, 8), 8)
            remote(
                own.at[it], cs[it].at[there], gs.at[it, i], gr.at[it, i], z_peers[i]
            ).wait_recv()

    def column_scale(it, s):
        return [cs[it][pl.ds(2 * col_of[s] + h, 1), :] for h in range(2)]

    row_total = jnp.zeros((8, LANES), jnp.float32)
    col_total = jnp.zeros((Z, 8, LANES), jnp.float32)
    for s in range(SLOTS):
        loads[s].wait()
        here = jnp.abs(tile[s])
        size[s] = here
        low, high = here[:, :LANES], here[:, LANES:]
        col_total = add_cols(
            col_total, s,
            [jnp.max(low, axis=0, keepdims=True), jnp.max(high, axis=0, keepdims=True)],
        )
        row_total = add_rows(row_total, s, row_peaks(low, high))
    colp[0] = col_total
    rowp[0] = row_total
    pl.semaphore_wait(barrier, len(FAR_Z) + 2 * len(FAR_8))
    sent = scatter_columns(0)
    send_rows(0)
    reduce_rows(0)
    part = reduce_chunk(0, sent)
    peak, y_sent = reduce_y(0, jnp.maximum(part, rowacc[...]))
    scale = 1.0 / jnp.sqrt(peak)

    spread_sent = spread(0, scale)
    rows_now = rs[0][...]
    for b in range(ROWB):
        for h in range(2):
            line = jnp.broadcast_to(rows_now[2 * b + h:2 * b + h + 1], (LANES, LANES))
            rsub[b, h * LANES:(h + 1) * LANES, :] = line.T
    col_total = jnp.zeros((Z, 8, LANES), jnp.float32)
    for s in range(SLOTS):
        here = size[s]
        left = rsub[row_of[s]]
        col_total = add_cols(
            col_total, s,
            [
                jnp.max(here[:, :LANES] * left, axis=0, keepdims=True),
                jnp.max(here[:, LANES:] * left, axis=0, keepdims=True),
            ],
        )
    colp[1] = col_total
    sent_2 = scatter_columns(1)
    await_columns(0, spread_sent)
    row_total = jnp.zeros((8, LANES), jnp.float32)
    for s in range(SLOTS):
        here = size[s]
        right = column_scale(0, s)
        row_total = add_rows(
            row_total, s, row_peaks(here[:, :LANES] * right[0], here[:, LANES:] * right[1])
        )
    rowp[1] = row_total
    send_rows(1)
    reduce_rows(1)
    part = reduce_chunk(1, sent_2)
    peak, y_sent_2 = reduce_y(1, jnp.maximum(part, rowacc[...]))
    scale = scale / jnp.sqrt(peak * scale)

    spread_sent_2 = spread(1, scale)
    rows_now = rs[1][...]
    for b in range(ROWB):
        for h in range(2):
            scaling_ref[b:b + 1, h * LANES:(h + 1) * LANES] = rows_now[2 * b + h:2 * b + h + 1]
    await_columns(1, spread_sent_2)
    for s in range(SLOTS):
        live = jnp.where(s < count, jnp.float32(1.0), jnp.float32(0.0))
        right = column_scale(1, s)
        for h in range(2):
            left = rs[1][pl.ds(2 * row_of[s] + h, 1), :]
            left_ref[s:s + 1, h * LANES:(h + 1) * LANES] = left * live
            right_ref[s:s + 1, h * LANES:(h + 1) * LANES] = right[h]

    for copy in sent + y_sent + spread_sent + sent_2 + y_sent_2 + spread_sent_2:
        copy.wait_send()
    for it in range(ITERS):
        @pl.when(owner)
        def _():
            for i in range(N - 1):
                scale_copy(it, i).wait_send()

        @pl.when(jnp.logical_not(owner))
        def _():
            row_copy(it, 0, (wide, y)).wait_send()


def on_device(tiles, tile_rows, tile_cols, tile_counts):
    smem = pl.BlockSpec(memory_space=pltpu.SMEM)
    vmem = pl.BlockSpec(memory_space=pltpu.VMEM)
    dma = pltpu.SemaphoreType.DMA
    chunk = (8, LANES)
    f32 = jnp.float32
    left, right, scaling = pl.pallas_call(
        kernel,
        name="equilibrate",
        out_shape=(
            jax.ShapeDtypeStruct((SLOTS, TILE), f32),
            jax.ShapeDtypeStruct((SLOTS, TILE), f32),
            jax.ShapeDtypeStruct((ROWB, TILE), f32),
        ),
        in_specs=[smem, smem, smem, pl.BlockSpec(memory_space=pl.ANY)],
        out_specs=(vmem, vmem, vmem),
        scratch_shapes=[
            pltpu.VMEM((SLOTS, TILE, TILE), f32),
            pltpu.VMEM((SLOTS, TILE, TILE), f32),
            pltpu.VMEM((ROWB, TILE, LANES), f32),
            pltpu.VMEM((ITERS, Z) + chunk, f32),
            pltpu.VMEM((ITERS,) + chunk, f32),
            pltpu.VMEM(chunk, f32),
            pltpu.VMEM((ITERS, N - 1) + chunk, f32),
            pltpu.VMEM((ITERS, Z - 1) + chunk, f32),
            pltpu.VMEM((ITERS,) + chunk, f32),
            pltpu.VMEM((ITERS, Y - 1) + chunk, f32),
            pltpu.VMEM((ITERS,) + chunk, f32),
            pltpu.VMEM((Z * 8, LANES), f32),
            pltpu.VMEM((Z * 8, LANES), f32),
            pltpu.VMEM(chunk, f32),
            pltpu.VMEM(chunk, f32),
            dma((SLOTS,)),
            dma((ITERS, Z - 1)), dma((ITERS, Z - 1)),
            dma((ITERS, Z - 1)), dma((ITERS, Z - 1)),
            dma((ITERS, Y - 1)), dma((ITERS, Y - 1)),
            dma((ITERS,)), dma((ITERS, N - 1)),
            dma((ITERS, N - 1)), dma((ITERS,)),
        ],
        compiler_params=pltpu.CompilerParams(collective_id=0, has_side_effects=True),
    )(tile_rows, tile_cols, tile_counts, tiles)
    result = tiles[0] * left[:, :, None] * right[:, None, :]
    return (result[None], scaling)


def solution(mesh):
    placed = (
        P("wide", "narrow", None, None),
        P("wide", "narrow"),
        P("wide", "narrow"),
        P("wide", "narrow"),
    )
    return jax.shard_map(
        on_device,
        mesh=mesh,
        in_specs=placed,
        out_specs=(P("wide", "narrow", None, None), P("wide", None)),
        check_vma=False,
    )
```

time: 622 us -> 64.1 us (0.10)
  waiting for transfers between devices: 506 us -> 0 us
  blocking collectives: 84.6 us -> 0 us
  Pallas kernels: 0 us -> 59 us
  between operations: 15 us -> 1.43 us
  other arithmetic: 9.81 us -> 2.13 us
    pmax x2 -> x0, waiting for transfers between devices: 506 us -> none  [on_device(): col_full = lax.pmax(col_part, 'wide')]
    pallas_call x0 -> x1, Pallas kernels: none -> 59 us  [on_device(): pl.pallas_call(kernel, name='equilibrate', out_shape=(jax.ShapeDtypeStruc...]
    psum x2 -> x0, blocking collectives: 46.3 us -> none  [from_root(): return lax.psum(block, axis)]
    pmax x2 -> x0, blocking collectives: 38.3 us -> none  [on_device(): row_full = lax.pmax(row_part, 'narrow')]
  transfers between devices with their start and end apart: 2 -> 0, of which waited for: 2 -> 0; matrix products, arithmetic and copies ran while one was open for 0% -> 0% of each run, Pallas kernels for 0% -> 0%
where the time goes in v1:
time: 64.1 us; the launch traced here: 63.2 us
  Pallas kernels  59 us (92%)
  other arithmetic  2.13 us (3%)
  between operations  1.43 us (2%)
    pallas_call x1, Pallas kernels, on_device(): pl.pallas_call(kernel, name='equilibrate', out_shape=(jax.ShapeDtypeStruc...  59 us
    mul x1, other arithmetic, on_device(): result = tiles[0] * left[:, :, None] * right[:, None, :]  2.13 us

profile of v1, /device:TPU:1, one launch (start us, length us, event | category | flops | bytes accessed | tf_op | source)
XLA Modules:
  0.0 63.2 jit_solution(8662680554904106428)
XLA Ops:
  0.6 0.0 copy-start
  1.4 59.0 %equilibrate.1 = (f32[6,256]{1,0:T(8,128)}, f32[6,256]{1,0:T(8,128)}, f32[4,256]{1,0:T(4,128)}) custom-call(s32[1,6]{1,0:T(1,128)} %rows_ref.1, s32[1,6]{1,0:T(1,128)} %cols_ref.1, s32[1,1]{1,0:T(1,128)S(6)} %copy.7.count_ref, f32[1,6,256,256]{3,2,1,0:T(8,128)} %tiles_ref.1), custom_call_target="tpu_custom_call" | custom-call | tf_op jit(solution)/shard_map/equilibrate/pallas_call | solution.py:283
  60.4 0.0 copy-done
  60.4 0.0 copy-start.1
  60.4 2.1 %multiply_multiply_fusion = f32[1,6,256,256]{3,2,1,0:T(8,128)} fusion(f32[1,6,256,256]{3,2,1,0:T(8,128)S(1)} %copy-done, f32[6,256]{1,0:T(8,128)} %get-tuple-element.6, f32[6,256]{1,0:T(8,128)} %get-tuple-element.5), kind=kLoop, calls=%fused_computation | loop fusion | flops 786432 | bytes 3158016 | tf_op jit(solution)/shard_map/mul | solution.py:318
  62.6 0.0 copy-done.1
  62.6 0.6 copy.8
Async XLA Ops:
  0.6 59.8 %copy-start = (f32[1,6,256,256]{3,2,1,0:T(8,128)S(1)}, f32[1,6,256,256]{3,2,1,0:T(8,128)}, u32[]{:S(2)}) copy-start(f32[1,6,256,256]{3,2,1,0:T(8,128)} %tiles_ref.1) | copy-start | bytes 4718596
  60.4 2.1 %copy-start.1 = (f32[4,256]{1,0:T(4,128)S(1)}, f32[4,256]{1,0:T(4,128)}, u32[]{:S(2)}) copy-start(f32[4,256]{1,0:T(4,128)} %get-tuple-element.11) | copy-start | bytes 12292

commit v2 on v1

--- a/solution.py
+++ b/solution.py
@@ -1,3 +1,5 @@
+import functools
+
 import jax
 import jax.numpy as jnp
 from jax import lax
@@ -47,10 +49,10 @@
 
 
 def kernel(
-    rows_ref, cols_ref, count_ref, tiles_ref,
+    rows_hbm, cols_hbm, count_ref, tiles_ref,
     left_ref, right_ref, scaling_ref,
-    tile, size, rsub, colp, rowp, rowacc, nrecv, zrecv, ypart, yrecv, own, cs_1, cs_2, rs_1, rs_2,
-    tsem, zs, zr, gs, gr, ys, yr, ns, nr, bs, br,
+    rows_ref, cols_ref, tile, size, rsub, colp, rowp, rowacc, nrecv, urecv, precv, zrecv, ypart, yrecv, own, cs_1, cs_2, rs_1, rs_2,
+    isem, tsem, zs, zr, gs, gr, ys, yr, ns, nr, bs, br, us, ur, ps, pr,
 ):
     wide, y, z, n = place()
     owner = n == y
@@ -59,9 +61,33 @@
     y_peers = [(lax.rem(y + d, Y) * Z + z, n) for d in FAR_8]
     n_peers = [(wide, lax.rem(n + d, N)) for d in FAR_8]
 
+    upper = n > y
+    chunk_users = [(n * Z + z, lax.rem(n + d, N)) for d in range(1, N)]
+    chunk_owners = [(to * Z + z, y) for to in range(Y)]
+
+    def each_user(step):
+        for i in range(N - 1):
+            pl.when(n + i + 1 < N)(functools.partial(step, i))
+
+    def signal(device):
+        pl.semaphore_signal(barrier, inc=1, device_id=device, device_id_type=MESH)
+
     barrier = pltpu.get_barrier_semaphore()
     for peer in z_peers + y_peers + n_peers:
-        pl.semaphore_signal(barrier, inc=1, device_id=peer, device_id_type=MESH)
+        signal(peer)
+    each_user(lambda i: signal(chunk_users[i]))
+
+    @pl.when(upper)
+    def _():
+        for device in chunk_owners:
+            signal(device)
+
+    integers = [
+        pltpu.make_async_copy(rows_hbm, rows_ref, isem.at[0]),
+        pltpu.make_async_copy(cols_hbm, cols_ref, isem.at[1]),
+    ]
+    for load in integers:
+        load.start()
     loads = [
         pltpu.make_async_copy(tiles_ref.at[0, s], tile.at[s], tsem.at[s])
         for s in range(SLOTS)
@@ -69,6 +95,8 @@
     for load in loads:
         load.start()
 
+    for load in integers:
+        load.wait()
     count = count_ref[0, 0]
     row_of = [
         jnp.clip(rows_ref[0, s] - wide * ROWB, 0, ROWB - 1) for s in range(SLOTS)
@@ -105,28 +133,62 @@
             copies.append(copy)
         return copies
 
-    def row_copy(it, slot, device):
-        return remote(
-            rowp.at[it], nrecv.at[it, slot], ns.at[it], nr.at[it, slot], device
-        )
-
-    def send_rows(it):
+    def row_copy(slot, device):
+        return remote(rowp.at[0], nrecv.at[slot], ns, nr.at[slot], device)
+
+    def send_rows():
         @pl.when(jnp.logical_not(owner))
         def _():
-            row_copy(it, lax.rem(n - y + N, N) - 1, (wide, y)).start()
-
-    def reduce_rows(it):
+            row_copy(lax.rem(n - y + N, N) - 1, (wide, y)).start()
+
+    def reduce_rows():
         @pl.when(owner)
         def _():
-            total = rowp[it]
+            total = rowp[0]
             for i in range(N - 1):
-                row_copy(it, i, n_peers[0]).wait_recv()
-                total = jnp.maximum(total, nrecv[it, i])
+                row_copy(i, n_peers[0]).wait_recv()
+                total = jnp.maximum(total, nrecv[i])
             rowacc[...] = total
 
         @pl.when(jnp.logical_not(owner))
         def _():
             rowacc[...] = jnp.zeros((8, LANES), jnp.float32)
+
+    def user_row_copy(to, slot):
+        return remote(
+            rowp.at[1], urecv.at[slot], us.at[to], ur.at[slot], chunk_owners[to]
+        )
+
+    def send_rows_to_owners():
+        @pl.when(upper)
+        def _():
+            for to in range(Y):
+                user_row_copy(to, n - y - 1).start()
+
+        rowacc[...] = jnp.where(owner, rowp[1], 0.0)
+
+    def reduce_user_rows():
+        def step(i):
+            user_row_copy(0, i).wait_recv()
+            rowacc[...] = jnp.maximum(rowacc[...], urecv[i])
+
+        each_user(step)
+
+    def part_copy(i, slot):
+        return remote(
+            ypart.at[0], precv.at[slot], ps.at[i], pr.at[slot], chunk_users[i]
+        )
+
+    def await_row_scale(scale):
+        rs[0][...] = scale
+
+        @pl.when(upper)
+        def _():
+            total = None
+            for i in range(Y):
+                part_copy(0, i).wait_recv()
+                total = precv[i] if total is None else jnp.maximum(total, precv[i])
+            rs[0][...] = 1.0 / jnp.sqrt(total)
 
     def reduce_chunk(it, copies):
         total = colp[it, z]
@@ -137,6 +199,8 @@
 
     def reduce_y(it, part):
         ypart[it] = part
+        if it == 0:
+            each_user(lambda i: part_copy(i, y).start())
         copies = []
         for i in range(Y - 1):
             copy = remote(
@@ -149,17 +213,18 @@
             part = jnp.maximum(part, yrecv[it, i])
         return part, copies
 
-    def scale_copy(it, i):
-        return remote(own.at[it], rs[it], bs.at[it, i], br.at[it], n_peers[i])
+    def scale_copy(i):
+        return remote(own.at[1], rs[1], bs.at[i], br, n_peers[i])
 
     def spread(it, scale):
         own[it] = scale
         mine = pl.ds(pl.multiple_of(z * 8, 8), 8)
 
-        @pl.when(owner)
-        def _():
-            for i in range(N - 1):
-                scale_copy(it, i).start()
+        if it == 1:
+            @pl.when(owner)
+            def _():
+                for i in range(N - 1):
+                    scale_copy(i).start()
 
         copies = []
         for i in range(Z - 1):
@@ -170,13 +235,16 @@
             copies.append(copy)
         cs[it][mine] = scale
 
-        @pl.when(owner)
-        def _():
-            rs[it][...] = scale
-
-        @pl.when(jnp.logical_not(owner))
-        def _():
-            scale_copy(it, 0).wait_recv()
+        if it == 1:
+            @pl.when(owner)
+            def _():
+                rs[1][...] = scale
+
+            @pl.when(jnp.logical_not(owner))
+            def _():
+                scale_copy(0).wait_recv()
+        else:
+            await_row_scale(scale)
 
         return copies
 
@@ -205,10 +273,12 @@
         row_total = add_rows(row_total, s, row_peaks(low, high))
     colp[0] = col_total
     rowp[0] = row_total
-    pl.semaphore_wait(barrier, len(FAR_Z) + 2 * len(FAR_8))
+    pl.semaphore_wait(
+        barrier, len(FAR_Z) + 2 * len(FAR_8) + N - 1 - n + jnp.where(upper, Y, 0)
+    )
     sent = scatter_columns(0)
-    send_rows(0)
-    reduce_rows(0)
+    send_rows()
+    reduce_rows()
     part = reduce_chunk(0, sent)
     peak, y_sent = reduce_y(0, jnp.maximum(part, rowacc[...]))
     scale = 1.0 / jnp.sqrt(peak)
@@ -241,10 +311,11 @@
             row_total, s, row_peaks(here[:, :LANES] * right[0], here[:, LANES:] * right[1])
         )
     rowp[1] = row_total
-    send_rows(1)
-    reduce_rows(1)
+    send_rows_to_owners()
     part = reduce_chunk(1, sent_2)
     peak, y_sent_2 = reduce_y(1, jnp.maximum(part, rowacc[...]))
+    reduce_user_rows()
+    peak = jnp.maximum(peak, rowacc[...])
     scale = scale / jnp.sqrt(peak * scale)
 
     spread_sent_2 = spread(1, scale)
@@ -263,21 +334,52 @@
 
     for copy in sent + y_sent + spread_sent + sent_2 + y_sent_2 + spread_sent_2:
         copy.wait_send()
-    for it in range(ITERS):
-        @pl.when(owner)
-        def _():
-            for i in range(N - 1):
-                scale_copy(it, i).wait_send()
-
-        @pl.when(jnp.logical_not(owner))
-        def _():
-            row_copy(it, 0, (wide, y)).wait_send()
+    each_user(lambda i: part_copy(i, y).wait_send())
+
+    @pl.when(owner)
+    def _():
+        for i in range(N - 1):
+            scale_copy(i).wait_send()
+
+    @pl.when(jnp.logical_not(owner))
+    def _():
+        row_copy(0, (wide, y)).wait_send()
+
+    @pl.when(upper)
+    def _():
+        for to in range(Y):
+            user_row_copy(to, 0).wait_send()
+
+
+def finish(tiles_ref, left_ref, right_ref, found_ref, result_ref, scaling_ref, done, sems):
+    copies = []
+    for s in range(SLOTS):
+        for h in range(2):
+            rows = slice(h * LANES, (h + 1) * LANES)
+            line = left_ref[s:s + 1, rows]
+            left = jnp.broadcast_to(line, (LANES, LANES)).T
+            for g in range(2):
+                cols = slice(g * LANES, (g + 1) * LANES)
+                done[s, rows, cols] = (
+                    tiles_ref[0, s, rows, cols] * left * right_ref[s:s + 1, cols]
+                )
+        copy = pltpu.make_async_copy(done.at[s], result_ref.at[0, s], sems.at[s])
+        copy.start()
+        copies.append(copy)
+    scaling_ref[...] = found_ref[...]
+    for copy in copies:
+        copy.wait()
 
 
 def on_device(tiles, tile_rows, tile_cols, tile_counts):
     smem = pl.BlockSpec(memory_space=pltpu.SMEM)
+    anywhere = pl.BlockSpec(memory_space=pltpu.HBM)
     vmem = pl.BlockSpec(memory_space=pltpu.VMEM)
     dma = pltpu.SemaphoreType.DMA
+
+    def held(given):
+        return pltpu.with_memory_space_constraint(given, pltpu.HBM)
+
     chunk = (8, LANES)
     f32 = jnp.float32
     left, right, scaling = pl.pallas_call(
@@ -288,16 +390,20 @@
             jax.ShapeDtypeStruct((SLOTS, TILE), f32),
             jax.ShapeDtypeStruct((ROWB, TILE), f32),
         ),
-        in_specs=[smem, smem, smem, pl.BlockSpec(memory_space=pl.ANY)],
+        in_specs=[anywhere, anywhere, smem, anywhere],
         out_specs=(vmem, vmem, vmem),
         scratch_shapes=[
+            pltpu.SMEM((1, SLOTS), jnp.int32),
+            pltpu.SMEM((1, SLOTS), jnp.int32),
             pltpu.VMEM((SLOTS, TILE, TILE), f32),
             pltpu.VMEM((SLOTS, TILE, TILE), f32),
             pltpu.VMEM((ROWB, TILE, LANES), f32),
             pltpu.VMEM((ITERS, Z) + chunk, f32),
             pltpu.VMEM((ITERS,) + chunk, f32),
             pltpu.VMEM(chunk, f32),
-            pltpu.VMEM((ITERS, N - 1) + chunk, f32),
+            pltpu.VMEM((N - 1,) + chunk, f32),
+            pltpu.VMEM((N - 1,) + chunk, f32),
+            pltpu.VMEM((Y,) + chunk, f32),
             pltpu.VMEM((ITERS, Z - 1) + chunk, f32),
             pltpu.VMEM((ITERS,) + chunk, f32),
             pltpu.VMEM((ITERS, Y - 1) + chunk, f32),
@@ -306,17 +412,31 @@
             pltpu.VMEM((Z * 8, LANES), f32),
             pltpu.VMEM(chunk, f32),
             pltpu.VMEM(chunk, f32),
-            dma((SLOTS,)),
+            dma((2,)), dma((SLOTS,)),
             dma((ITERS, Z - 1)), dma((ITERS, Z - 1)),
             dma((ITERS, Z - 1)), dma((ITERS, Z - 1)),
             dma((ITERS, Y - 1)), dma((ITERS, Y - 1)),
-            dma((ITERS,)), dma((ITERS, N - 1)),
-            dma((ITERS, N - 1)), dma((ITERS,)),
+            dma, dma((N - 1,)),
+            dma((N - 1,)), dma,
+            dma((Y,)), dma((N - 1,)),
+            dma((N - 1,)), dma((Y,)),
         ],
-        compiler_params=pltpu.CompilerParams(collective_id=0, has_side_effects=True),
-    )(tile_rows, tile_cols, tile_counts, tiles)
-    result = tiles[0] * left[:, :, None] * right[:, None, :]
-    return (result[None], scaling)
+        compiler_params=pltpu.CompilerParams(
+            collective_id=0, has_side_effects=True, vmem_limit_bytes=16 << 20
+        ),
+    )(held(tile_rows), held(tile_cols), tile_counts, held(tiles))
+    return pl.pallas_call(
+        finish,
+        name="finish",
+        out_shape=(
+            jax.ShapeDtypeStruct((1, SLOTS, TILE, TILE), f32),
+            jax.ShapeDtypeStruct((ROWB, TILE), f32),
+        ),
+        in_specs=[vmem, vmem, vmem, vmem],
+        out_specs=(anywhere, vmem),
+        scratch_shapes=[pltpu.VMEM((SLOTS, TILE, TILE), f32), dma((SLOTS,))],
+        compiler_params=pltpu.CompilerParams(vmem_limit_bytes=8 << 20),
+    )(tiles, left, right, scaling)
 
 
 def solution(mesh):

time: 64.1 us -> 60.1 us (0.938); the launches traced: 63.2 us -> 60 us
  other arithmetic: 2.13 us -> 0 us
    pallas_call x1, Pallas kernels: 59 us -> 56.7 us  [on_device(): pl.pallas_call(kernel, name='equilibrate', out_shape=(jax.ShapeDtypeStruc...]
    mul x1 -> x0, other arithmetic: 2.13 us -> none  [on_device(): result = tiles[0] * left[:, :, None] * right[:, None, :]]
    pallas_call x0 -> x1, Pallas kernels: none -> 1.88 us  [on_device(): pl.pallas_call(finish, name='finish', out_shape=(jax.ShapeDtypeStruct((1,...]
where the time goes in v2:
time: 60.1 us; the launch traced here: 60 us
  Pallas kernels  58.5 us (97%)
  between operations  1.42 us (2%)
    pallas_call x1, Pallas kernels, on_device(): pl.pallas_call(kernel, name='equilibrate', out_shape=(jax.ShapeDtypeStruc...  56.7 us
    pallas_call x1, Pallas kernels, on_device(): pl.pallas_call(finish, name='finish', out_shape=(jax.ShapeDtypeStruct((1,...  1.88 us

profile of v2, /device:TPU:1, one launch (start us, length us, event | category | flops | bytes accessed | tf_op | source)
XLA Modules:
  0.0 60.0 jit_solution(1203156279035889569)
XLA Ops:
  0.6 0.0 copy-start
  1.4 56.7 %equilibrate.1 = (f32[6,256]{1,0:T(8,128)S(1)}, f32[6,256]{1,0:T(8,128)S(1)}, f32[4,256]{1,0:T(4,128)S(1)}) custom-call(s32[1,6]{1,0:T(1,128)} %rows_hbm.1, s32[1,6]{1,0:T(1,128)} %cols_hbm.1, s32[1,1]{1,0:T(1,128)S(6)} %copy.6.count_ref, f32[1,6,256,256]{3,2,1,0:T(8,128)} %tiles_ref.3), custom_call_target="tpu_custom_call" | custom-call | tf_op jit(solution)/shard_map/equilibrate/pallas_call | solution.py:385
  58.1 0.0 copy-done
  58.1 1.9 %finish.1 = (f32[1,6,256,256]{3,2,1,0:T(8,128)}, f32[4,256]{1,0:T(4,128)}) custom-call(f32[1,6,256,256]{3,2,1,0:T(8,128)S(1)} %copy-done, f32[6,256]{1,0:T(8,128)S(1)} %get-tuple-element.5.left_ref, f32[6,256]{1,0:T(8,128)S(1)} %get-tuple-element.6.right_ref, f32[4,256]{1,0:T(4,128)S(1)} %get-tuple-element.7.found_ref), custom_call_target="tpu_custom_call" | custom-call | tf_op jit(solution)/shard_map/finish/pallas_call | solution.py:428
Async XLA Ops:
  0.6 57.4 %copy-start = (f32[1,6,256,256]{3,2,1,0:T(8,128)S(1)}, f32[1,6,256,256]{3,2,1,0:T(8,128)}, u32[]{:S(2)}) copy-start(f32[1,6,256,256]{3,2,1,0:T(8,128)} %tiles_ref.3) | copy-start | bytes 4718596

commit v3 on v2

--- a/solution.py
+++ b/solution.py
@@ -67,7 +67,11 @@
 
     def each_user(step):
         for i in range(N - 1):
-            pl.when(n + i + 1 < N)(functools.partial(step, i))
+            pl.when(jnp.logical_and(y <= n, n + i + 1 < N))(functools.partial(step, i))
+
+    def each_owner(step):
+        for to in range(Y):
+            pl.when(jnp.logical_and(n > y, to <= y))(functools.partial(step, to))
 
     def signal(device):
         pl.semaphore_signal(barrier, inc=1, device_id=device, device_id_type=MESH)
@@ -77,11 +81,7 @@
         signal(peer)
     each_user(lambda i: signal(chunk_users[i]))
 
-    @pl.when(upper)
-    def _():
-        for device in chunk_owners:
-            signal(device)
-
+    each_owner(lambda to: signal(chunk_owners[to]))
     integers = [
         pltpu.make_async_copy(rows_hbm, rows_ref, isem.at[0]),
         pltpu.make_async_copy(cols_hbm, cols_ref, isem.at[1]),
@@ -160,11 +160,7 @@
         )
 
     def send_rows_to_owners():
-        @pl.when(upper)
-        def _():
-            for to in range(Y):
-                user_row_copy(to, n - y - 1).start()
-
+        each_owner(lambda to: user_row_copy(to, n - y - 1).start())
         rowacc[...] = jnp.where(owner, rowp[1], 0.0)
 
     def reduce_user_rows():
@@ -181,14 +177,17 @@
 
     def await_row_scale(scale):
         rs[0][...] = scale
+        rowacc[...] = jnp.zeros((8, LANES), jnp.float32)
+
+        def step(i):
+            part_copy(0, i).wait_recv()
+            rowacc[...] = jnp.maximum(rowacc[...], precv[i])
+
+        each_owner(step)
 
         @pl.when(upper)
         def _():
-            total = None
-            for i in range(Y):
-                part_copy(0, i).wait_recv()
-                total = precv[i] if total is None else jnp.maximum(total, precv[i])
-            rs[0][...] = 1.0 / jnp.sqrt(total)
+            rs[0][...] = 1.0 / jnp.sqrt(rowacc[...])
 
     def reduce_chunk(it, copies):
         total = colp[it, z]
@@ -259,6 +258,13 @@
     def column_scale(it, s):
         return [cs[it][pl.ds(2 * col_of[s] + h, 1), :] for h in range(2)]
 
+    def spread_rows(it):
+        now = rs[it][...]
+        for b in range(ROWB):
+            for h in range(2):
+                line = jnp.broadcast_to(now[2 * b + h:2 * b + h + 1], (LANES, LANES))
+                rsub[b, h * LANES:(h + 1) * LANES, :] = line.T
+
     row_total = jnp.zeros((8, LANES), jnp.float32)
     col_total = jnp.zeros((Z, 8, LANES), jnp.float32)
     for s in range(SLOTS):
@@ -274,7 +280,9 @@
     colp[0] = col_total
     rowp[0] = row_total
     pl.semaphore_wait(
-        barrier, len(FAR_Z) + 2 * len(FAR_8) + N - 1 - n + jnp.where(upper, Y, 0)
+        barrier,
+        len(FAR_Z) + 2 * len(FAR_8)
+        + jnp.where(y <= n, N - 1 - n, 0) + jnp.where(upper, y + 1, 0),
     )
     sent = scatter_columns(0)
     send_rows()
@@ -284,11 +292,7 @@
     scale = 1.0 / jnp.sqrt(peak)
 
     spread_sent = spread(0, scale)
-    rows_now = rs[0][...]
-    for b in range(ROWB):
-        for h in range(2):
-            line = jnp.broadcast_to(rows_now[2 * b + h:2 * b + h + 1], (LANES, LANES))
-            rsub[b, h * LANES:(h + 1) * LANES, :] = line.T
+    spread_rows(0)
     col_total = jnp.zeros((Z, 8, LANES), jnp.float32)
     for s in range(SLOTS):
         here = size[s]
@@ -323,13 +327,16 @@
     for b in range(ROWB):
         for h in range(2):
             scaling_ref[b:b + 1, h * LANES:(h + 1) * LANES] = rows_now[2 * b + h:2 * b + h + 1]
+    spread_rows(1)
+    for s in range(SLOTS):
+        left = rsub[row_of[s]]
+        for h in range(2):
+            cols = slice(h * LANES, (h + 1) * LANES)
+            left_ref[s, :, cols] = jnp.where(s < count, tile[s, :, cols] * left, 0.0)
     await_columns(1, spread_sent_2)
     for s in range(SLOTS):
-        live = jnp.where(s < count, jnp.float32(1.0), jnp.float32(0.0))
         right = column_scale(1, s)
         for h in range(2):
-            left = rs[1][pl.ds(2 * row_of[s] + h, 1), :]
-            left_ref[s:s + 1, h * LANES:(h + 1) * LANES] = left * live
             right_ref[s:s + 1, h * LANES:(h + 1) * LANES] = right[h]
 
     for copy in sent + y_sent + spread_sent + sent_2 + y_sent_2 + spread_sent_2:
@@ -345,28 +352,23 @@
     def _():
         row_copy(0, (wide, y)).wait_send()
 
-    @pl.when(upper)
-    def _():
-        for to in range(Y):
-            user_row_copy(to, 0).wait_send()
-
-
-def finish(tiles_ref, left_ref, right_ref, found_ref, result_ref, scaling_ref, done, sems):
+    each_owner(lambda to: user_row_copy(to, 0).wait_send())
+
+
+def finish(left_ref, right_ref, found_ref, result_ref, scaling_ref, done, sems, found_sem):
+    found = pltpu.make_async_copy(found_ref, scaling_ref, found_sem)
+    found.start()
     copies = []
     for s in range(SLOTS):
         for h in range(2):
             rows = slice(h * LANES, (h + 1) * LANES)
-            line = left_ref[s:s + 1, rows]
-            left = jnp.broadcast_to(line, (LANES, LANES)).T
-            for g in range(2):
-                cols = slice(g * LANES, (g + 1) * LANES)
-                done[s, rows, cols] = (
-                    tiles_ref[0, s, rows, cols] * left * right_ref[s:s + 1, cols]
-                )
-        copy = pltpu.make_async_copy(done.at[s], result_ref.at[0, s], sems.at[s])
-        copy.start()
-        copies.append(copy)
-    scaling_ref[...] = found_ref[...]
+            done[s, rows] = left_ref[s, rows] * right_ref[s:s + 1, :]
+            copy = pltpu.make_async_copy(
+                done.at[s, rows], result_ref.at[0, s, rows], sems.at[s, h]
+            )
+            copy.start()
+            copies.append(copy)
+    found.wait()
     for copy in copies:
         copy.wait()
 
@@ -386,7 +388,7 @@
         kernel,
         name="equilibrate",
         out_shape=(
-            jax.ShapeDtypeStruct((SLOTS, TILE), f32),
+            jax.ShapeDtypeStruct((SLOTS, TILE, TILE), f32),
             jax.ShapeDtypeStruct((SLOTS, TILE), f32),
             jax.ShapeDtypeStruct((ROWB, TILE), f32),
         ),
@@ -432,11 +434,11 @@
             jax.ShapeDtypeStruct((1, SLOTS, TILE, TILE), f32),
             jax.ShapeDtypeStruct((ROWB, TILE), f32),
         ),
-        in_specs=[vmem, vmem, vmem, vmem],
-        out_specs=(anywhere, vmem),
-        scratch_shapes=[pltpu.VMEM((SLOTS, TILE, TILE), f32), dma((SLOTS,))],
+        in_specs=[vmem, vmem, vmem],
+        out_specs=(anywhere, anywhere),
+        scratch_shapes=[pltpu.VMEM((SLOTS, TILE, TILE), f32), dma((SLOTS, 2)), dma],
         compiler_params=pltpu.CompilerParams(vmem_limit_bytes=8 << 20),
-    )(tiles, left, right, scaling)
+    )(left, right, scaling)
 
 
 def solution(mesh):

time: 60.1 us -> 59 us (0.982)
  Pallas kernels: 58.5 us -> 57.6 us
    pallas_call x1, Pallas kernels: 1.88 us -> 1.25 us  [on_device(): pl.pallas_call(finish, name='finish', out_shape=(jax.ShapeDtypeStruct((1,...]
where the time goes in v3:
time: 59 us; the launch traced here: 58.8 us
  Pallas kernels  57.6 us (98%)
  between operations  1.29 us (2%)
    pallas_call x1, Pallas kernels, on_device(): pl.pallas_call(kernel, name='equilibrate', out_shape=(jax.ShapeDtypeStruc...  56.3 us
    pallas_call x1, Pallas kernels, on_device(): pl.pallas_call(finish, name='finish', out_shape=(jax.ShapeDtypeStruct((1,...  1.25 us

profile of v3, /device:TPU:1, one launch (start us, length us, event | category | flops | bytes accessed | tf_op | source)
XLA Modules:
  0.0 58.8 jit_solution(7014839328016634407)
XLA Ops:
  1.3 56.3 %equilibrate.1 = (f32[6,256,256]{2,1,0:T(8,128)S(1)}, f32[6,256]{1,0:T(8,128)S(1)}, f32[4,256]{1,0:T(4,128)S(1)}) custom-call(s32[1,6]{1,0:T(1,128)} %rows_hbm.1, s32[1,6]{1,0:T(1,128)} %cols_hbm.1, s32[1,1]{1,0:T(1,128)S(6)} %copy.6.count_ref, f32[1,6,256,256]{3,2,1,0:T(8,128)} %tiles_ref.1), custom_call_target="tpu_custom_call" | custom-call | tf_op jit(solution)/shard_map/equilibrate/pallas_call | solution.py:387
  57.6 1.3 %finish.1 = (f32[1,6,256,256]{3,2,1,0:T(8,128)}, f32[4,256]{1,0:T(4,128)}) custom-call(f32[6,256,256]{2,1,0:T(8,128)S(1)} %get-tuple-element.5.left_ref, f32[6,256]{1,0:T(8,128)S(1)} %get-tuple-element.6.right_ref, f32[4,256]{1,0:T(4,128)S(1)} %get-tuple-element.7.found_ref), custom_call_target="tpu_custom_call" | custom-call | tf_op jit(solution)/shard_map/finish/pallas_call | solution.py:430

commit v4 on v3

--- a/solution.py
+++ b/solution.py
@@ -333,12 +333,6 @@
         for h in range(2):
             cols = slice(h * LANES, (h + 1) * LANES)
             left_ref[s, :, cols] = jnp.where(s < count, tile[s, :, cols] * left, 0.0)
-    await_columns(1, spread_sent_2)
-    for s in range(SLOTS):
-        right = column_scale(1, s)
-        for h in range(2):
-            right_ref[s:s + 1, h * LANES:(h + 1) * LANES] = right[h]
-
     for copy in sent + y_sent + spread_sent + sent_2 + y_sent_2 + spread_sent_2:
         copy.wait_send()
     each_user(lambda i: part_copy(i, y).wait_send())
@@ -353,6 +347,12 @@
         row_copy(0, (wide, y)).wait_send()
 
     each_owner(lambda to: user_row_copy(to, 0).wait_send())
+
+    await_columns(1, spread_sent_2)
+    for s in range(SLOTS):
+        right = column_scale(1, s)
+        for h in range(2):
+            right_ref[s:s + 1, h * LANES:(h + 1) * LANES] = right[h]
 
 
 def finish(left_ref, right_ref, found_ref, result_ref, scaling_ref, done, sems, found_sem):

time: 59 us -> 58.8 us (level)
  no operation moved by 1% of the time
where the time goes in v4:
time: 58.8 us; the launch traced here: 58.7 us
  Pallas kernels  57.4 us (98%)
  between operations  1.29 us (2%)
    pallas_call x1, Pallas kernels, on_device(): pl.pallas_call(kernel, name='equilibrate', out_shape=(jax.ShapeDtypeStruc...  56.1 us
    pallas_call x1, Pallas kernels, on_device(): pl.pallas_call(finish, name='finish', out_shape=(jax.ShapeDtypeStruct((1,...  1.25 us

profile of v4, /device:TPU:1, one launch (start us, length us, event | category | flops | bytes accessed | tf_op | source)
XLA Modules:
  0.0 58.7 jit_solution(976888187224967843)
XLA Ops:
  1.3 56.1 %equilibrate.1 = (f32[6,256,256]{2,1,0:T(8,128)S(1)}, f32[6,256]{1,0:T(8,128)S(1)}, f32[4,256]{1,0:T(4,128)S(1)}) custom-call(s32[1,6]{1,0:T(1,128)} %rows_hbm.1, s32[1,6]{1,0:T(1,128)} %cols_hbm.1, s32[1,1]{1,0:T(1,128)S(6)} %copy.6.count_ref, f32[1,6,256,256]{3,2,1,0:T(8,128)} %tiles_ref.1), custom_call_target="tpu_custom_call" | custom-call | tf_op jit(solution)/shard_map/equilibrate/pallas_call | solution.py:387
  57.4 1.3 %finish.1 = (f32[1,6,256,256]{3,2,1,0:T(8,128)}, f32[4,256]{1,0:T(4,128)}) custom-call(f32[6,256,256]{2,1,0:T(8,128)S(1)} %get-tuple-element.5.left_ref, f32[6,256]{1,0:T(8,128)S(1)} %get-tuple-element.6.right_ref, f32[4,256]{1,0:T(4,128)S(1)} %get-tuple-element.7.found_ref), custom_call_target="tpu_custom_call" | custom-call | tf_op jit(solution)/shard_map/finish/pallas_call | solution.py:430

commit v5 on v4

--- a/solution.py
+++ b/solution.py
@@ -198,8 +198,6 @@
 
     def reduce_y(it, part):
         ypart[it] = part
-        if it == 0:
-            each_user(lambda i: part_copy(i, y).start())
         copies = []
         for i in range(Y - 1):
             copy = remote(
@@ -207,6 +205,8 @@
             )
             copy.start()
             copies.append(copy)
+        if it == 0:
+            each_user(lambda i: part_copy(i, y).start())
         for i, copy in enumerate(copies):
             copy.wait_recv()
             part = jnp.maximum(part, yrecv[it, i])

time: 58.8 us -> 58.9 us (level)
  no operation moved by 1% of the time
where the time goes in v5:
time: 58.9 us; the launch traced here: 58.5 us
  Pallas kernels  57.2 us (97%)
  between operations  1.29 us (2%)
    pallas_call x1, Pallas kernels, on_device(): pl.pallas_call(kernel, name='equilibrate', out_shape=(jax.ShapeDtypeStruc...  56 us
    pallas_call x1, Pallas kernels, on_device(): pl.pallas_call(finish, name='finish', out_shape=(jax.ShapeDtypeStruct((1,...  1.25 us

profile of v5, /device:TPU:1, one launch (start us, length us, event | category | flops | bytes accessed | tf_op | source)
XLA Modules:
  0.0 58.5 jit_solution(9614885059023561331)
XLA Ops:
  1.3 56.0 %equilibrate.1 = (f32[6,256,256]{2,1,0:T(8,128)S(1)}, f32[6,256]{1,0:T(8,128)S(1)}, f32[4,256]{1,0:T(4,128)S(1)}) custom-call(s32[1,6]{1,0:T(1,128)} %rows_hbm.1, s32[1,6]{1,0:T(1,128)} %cols_hbm.1, s32[1,1]{1,0:T(1,128)S(6)} %copy.6.count_ref, f32[1,6,256,256]{3,2,1,0:T(8,128)} %tiles_ref.1), custom_call_target="tpu_custom_call" | custom-call | tf_op jit(solution)/shard_map/equilibrate/pallas_call | solution.py:387
  57.3 1.3 %finish.1 = (f32[1,6,256,256]{3,2,1,0:T(8,128)}, f32[4,256]{1,0:T(4,128)}) custom-call(f32[6,256,256]{2,1,0:T(8,128)S(1)} %get-tuple-element.5.left_ref, f32[6,256]{1,0:T(8,128)S(1)} %get-tuple-element.6.right_ref, f32[4,256]{1,0:T(4,128)S(1)} %get-tuple-element.7.found_ref), custom_call_target="tpu_custom_call" | custom-call | tf_op jit(solution)/shard_map/finish/pallas_call | solution.py:430
